TPU v7x, 512 devices: a whole 4x4x16 slice. The times are simulated.
512 devices in a mesh: loop: 64 (over z_lo, x, core), rep: 8 (over y, z_hi).
Axes of the slice: x: 4, y: 4, z: 16 (z_hi: 2, z_lo: 8; z = z_hi * 8 + z_lo), core: 2. Of those that a mesh axis runs over, the one named last changes fastest.
Arguments:
- features: bfloat16 [65536, 256], P(('loop', 'rep')), may hold values from -6 to 6
- weight: bfloat16 [256, 256], replicated, may hold values from -0.375 to 0.375
- tile_values: bfloat16 [49152, 128, 128], P(('loop', 'rep')), may hold values from -0.375 to 0.375
- tile_coords: int32 [49152, 2], P(('loop', 'rep')), may hold values from 0 to 7
- tile_counts: int32 [512, 8], P(('loop', 'rep')), may hold values from 1 to 12, as said below
Outputs:
- activated: bfloat16 [65536, 256], P(('loop', 'rep'))
Inputs may be any that keep to these rules, and one draw needn't show every extreme that they name: `tile_counts`: some list uses all 12 slots at some step; loads differ strongly between lists. `tile_coords`: row block within the group's rows and column block within the slab of that step.
All inputs are finite; a program needn't handle non-finite values.
Results may differ from a plain program's by a relative error of at most 0.0049.
Values may be sent and summed in bfloat16 or wider, within the bound.
A program may use at most 64 MiB of HBM per device.

v0:
```python
import jax
import jax.numpy as jnp
from jax import lax
from jax.sharding import PartitionSpec as P


def from_behind(x, axis, by):
    count = lax.axis_size(axis)
    return lax.ppermute(x, axis, [(i, (i + by) % count) for i in range(count)])


def local(features, weight, tile_values, tile_coords, tile_counts):
    rep_size = lax.axis_size("rep")
    loop_size = lax.axis_size("loop")
    step_count = loop_size // rep_size
    tile_size = tile_values.shape[1]
    feat_width = features.shape[1]
    slot_count = tile_values.shape[0] // step_count
    current_slab = lax.all_gather(features, "rep", axis=0, tiled=True)
    block_count = current_slab.shape[0] // tile_size
    values = tile_values.reshape(step_count, slot_count, tile_size, tile_size)
    coords = tile_coords.reshape(step_count, slot_count, 2)
    counts = tile_counts.reshape(step_count)
    rep_rank = lax.axis_index("rep")
    for bit_index in range(rep_size.bit_length() - 1):
        shifted = from_behind(current_slab, "loop", step_count * (1 << bit_index))
        current_slab = jnp.where(rep_rank >> bit_index & 1 == 1, shifted, current_slab)
    running = jnp.zeros((block_count, tile_size, feat_width), jnp.float32)
    for step_index in range(step_count):
        slab_blocks = current_slab.reshape(block_count, tile_size, feat_width)
        pieces = jnp.take(slab_blocks, coords[step_index, :, 1], axis=0)
        products = jnp.einsum(
            "ktc,kcf->ktf", values[step_index], pieces, preferred_element_type=jnp.float32
        )
        live_slot = (jnp.arange(slot_count) < counts[step_index]).astype(jnp.float32)
        running = running.at[coords[step_index, :, 0]].add(products * live_slot[:, None, None])
        if step_index + 1 < step_count:
            current_slab = from_behind(current_slab, "loop", 1)
    summed = lax.psum_scatter(
        running.reshape(block_count * tile_size, feat_width), "rep", scatter_dimension=0, tiled=True
    )
    aggregated = summed.astype(jnp.bfloat16)
    product = jnp.dot(aggregated, weight, preferred_element_type=jnp.float32)
    return jnp.maximum(product, 0.0).astype(jnp.bfloat16)


def solution(mesh):
    placed = (
        P(("loop", "rep"), None),
        P(),
        P(("loop", "rep"), None, None),
        P(("loop", "rep"), None),
        P(("loop", "rep"), None),
    )
    return jax.shard_map(
        local, mesh=mesh, in_specs=placed, out_specs=P(("loop", "rep"), None), check_vma=False
    )
```

profile of v0, /device:TPU:2, one launch (start us, length us, event | category | flops | bytes accessed | tf_op | source)
XLA Modules:
  0.0 455.2 jit_solution(15041202940088888313)
XLA Ops:
  6.5 90.3 %all_gather.3 = bf16[1024,256]{1,0:T(8,128)(2,1)S(1)} all-gather(bf16[128,256]{1,0:T(8,128)(2,1)} %param.7), channel_id=1, replica_groups=mesh['loop'=64,'rep'=8] {'rep'}, dimensions={0}, use_global_device_ids=true | all-gather | bytes 589824 | tf_op jit(solution)/shard_map/all_gather | solution.py:19
  96.8 6.3 %collective-permute-start = (bf16[1024,256]{1,0:T(8,128)(2,1)S(1)}, bf16[1024,256]{1,0:T(8,128)(2,1)S(1)}, u32[]{:S(2)}, u32[]{:S(2)}) collective-permute-start(bf16[1024,256]{1,0:T(8,128)(2,1)S(1)} %all_gather.3), channel_id=1, source_target_pairs={{0,64},{8,72},{16,80},{24,88},{32,96},{40,104},{48,112},{56,120},{... | collective-permute-start | bytes 1572872 | tf_op jit(solution)/shard_map/ppermute | solution.py:9
  103.2 12.8 %collective-permute-done = bf16[1024,256]{1,0:T(8,128)(2,1)S(1)} collective-permute-done((bf16[1024,256]{1,0:T(8,128)(2,1)S(1)}, bf16[1024,256]{1,0:T(8,128)(2,1)S(1)}, u32[]{:S(2)}, u32[]{:S(2)}) %collective-permute-start) | collective-permute-done | bytes 524320 | tf_op jit(solution)/shard_map/ppermute | solution.py:9
  116.0 5.9 %collective-permute-start.1 = (bf16[1024,256]{1,0:T(8,128)(2,1)S(1)}, bf16[1024,256]{1,0:T(8,128)(2,1)S(1)}, u32[]{:S(2)}, u32[]{:S(2)}) collective-permute-start(bf16[1024,256]{1,0:T(8,128)(2,1)S(1)} %broadcast_select_fusion), channel_id=1, source_target_pairs={{0,128},{8,136},{16,144},{24,152},{32,160},{40,168},{48,176},{56,1... | collective-permute-start | bytes 1572872 | tf_op jit(solution)/shard_map/ppermute | solution.py:9
  122.0 28.9 %collective-permute-done.1 = bf16[1024,256]{1,0:T(8,128)(2,1)S(1)} collective-permute-done((bf16[1024,256]{1,0:T(8,128)(2,1)S(1)}, bf16[1024,256]{1,0:T(8,128)(2,1)S(1)}, u32[]{:S(2)}, u32[]{:S(2)}) %collective-permute-start.1) | collective-permute-done | bytes 524320 | tf_op jit(solution)/shard_map/ppermute | solution.py:9
  150.9 2.7 collective-permute-start.2
  153.7 0.7 fusion.50
  154.4 0.6 compare_convert_fusion.7
  155.0 1.2 compare_convert_fusion.6
  156.2 16.9 %collective-permute-done.2 = bf16[1024,256]{1,0:T(8,128)(2,1)S(1)} collective-permute-done((bf16[1024,256]{1,0:T(8,128)(2,1)S(1)}, bf16[1024,256]{1,0:T(8,128)(2,1)S(1)}, u32[]{:S(2)}, u32[]{:S(2)}) %collective-permute-start.2) | collective-permute-done | bytes 524320 | tf_op jit(solution)/shard_map/ppermute | solution.py:9
  173.2 1.9 collective-permute-start.3
  175.1 1.2 compare_convert_fusion.5
  176.3 1.1 compare_convert_fusion.4
  177.4 1.2 compare_convert_fusion.3
  179.3 6.8 %collective-permute-done.3 = bf16[1024,256]{1,0:T(8,128)(2,1)S(1)} collective-permute-done((bf16[1024,256]{1,0:T(8,128)(2,1)S(1)}, bf16[1024,256]{1,0:T(8,128)(2,1)S(1)}, u32[]{:S(2)}, u32[]{:S(2)}) %collective-permute-start.3) | collective-permute-done | bytes 524320 | tf_op jit(solution)/shard_map/ppermute | solution.py:9
  186.1 1.9 collective-permute-start.4
  188.0 1.2 compare_convert_fusion.2
  191.0 5.6 %collective-permute-done.4 = bf16[1024,256]{1,0:T(8,128)(2,1)S(1)} collective-permute-done((bf16[1024,256]{1,0:T(8,128)(2,1)S(1)}, bf16[1024,256]{1,0:T(8,128)(2,1)S(1)}, u32[]{:S(2)}, u32[]{:S(2)}) %collective-permute-start.4) | collective-permute-done | bytes 524320 | tf_op jit(solution)/shard_map/ppermute | solution.py:9
  196.6 1.9 collective-permute-start.5
  198.5 1.1 compare_convert_fusion.1
  199.6 12.5 %collective-permute-done.5 = bf16[1024,256]{1,0:T(8,128)(2,1)} collective-permute-done((bf16[1024,256]{1,0:T(8,128)(2,1)S(1)}, bf16[1024,256]{1,0:T(8,128)(2,1)}, u32[]{:S(2)}, u32[]{:S(2)}) %collective-permute-start.5) | collective-permute-done | bytes 524320 | tf_op jit(solution)/shard_map/ppermute | solution.py:9
  212.1 1.9 collective-permute-start.6
  214.0 1.1 compare_convert_fusion
  216.4 2.6 multiply_bitcast_fusion.7
  219.0 1.9 copy.33
  221.0 1.8 scatter_fusion
  222.8 1.8 gather_fusion.1
  224.6 7.1 %collective-permute-done.6 = bf16[1024,256]{1,0:T(8,128)(2,1)} collective-permute-done((bf16[1024,256]{1,0:T(8,128)(2,1)}, bf16[1024,256]{1,0:T(8,128)(2,1)}, u32[]{:S(2)}, u32[]{:S(2)}) %collective-permute-start.6) | collective-permute-done | bytes 524320 | tf_op jit(solution)/shard_map/ppermute | solution.py:9
  231.7 1.9 collective-permute-start.7
  233.6 1.5 multiply_bitcast_fusion.6
  235.1 1.6 copy.37
  236.7 3.1 scatter_fusion.1
  239.8 0.7 gather_fusion.2
  240.6 1.5 multiply_bitcast_fusion.5
  242.1 1.6 copy.41
  243.7 3.1 scatter_fusion.2
  246.8 1.8 gather_fusion.3
  248.6 2.6 collective-permute-done.7
  251.2 2.1 collective-permute-start.8
  253.3 1.5 multiply_bitcast_fusion.4
  254.8 1.6 copy.45
  256.4 3.1 scatter_fusion.3
  259.5 1.6 gather_fusion.4
  261.2 1.5 multiply_bitcast_fusion.3
  262.7 1.6 copy.49
  264.3 3.1 scatter_fusion.4
  267.4 1.6 gather_fusion.5
  269.1 1.6 collective-permute-done.8
  270.7 1.9 collective-permute-start.9
  272.6 1.5 multiply_bitcast_fusion.2
  274.1 1.6 copy.53
  275.7 3.1 scatter_fusion.5
  278.9 1.6 gather_fusion.6
  280.6 1.5 multiply_bitcast_fusion.1
  282.1 1.6 copy.57
  283.7 3.1 scatter_fusion.6
  286.8 3.4 collective-permute-done.9
  290.2 1.6 gather_fusion.7
  291.9 2.6 multiply_bitcast_fusion
  294.5 1.9 copy.61
  296.4 1.8 scatter_fusion.7
  298.3 1.0 copy-done.1
  299.2 147.4 %reduce-scatter.2.cloned.1.call-done = f32[128,256]{1,0:T(8,128)} async-done(((f32[1024,256]{1,0:T(8,128)}), f32[128,256]{1,0:T(8,128)}) %reduce-scatter.2.cloned.1.call-update) | async-done | bytes 131088 | tf_op jit(solution)/shard_map/reduce_scatter | solution.py:39
  446.7 1.7 fusion
  (55 shorter events, 4.0 us)
Async XLA Ops:
  6.5 440.1 %copy-start = (bf16[256,256]{1,0:T(8,128)(2,1)S(1)}, bf16[256,256]{1,0:T(8,128)(2,1)}, u32[]{:S(2)}) copy-start(bf16[256,256]{1,0:T(8,128)(2,1)} %param.8) | copy-start | bytes 393220
  6.5 440.1 %reduce-scatter.2.cloned.1.call-start = ((), (), s32[]{:S(2)}) async-start(), calls=%async_computation.1 | async-start | bytes 1179648 | tf_op jit(solution)/shard_map/reduce_scatter | solution.py:39
  96.8 19.1 %collective-permute-start = (bf16[1024,256]{1,0:T(8,128)(2,1)S(1)}, bf16[1024,256]{1,0:T(8,128)(2,1)S(1)}, u32[]{:S(2)}, u32[]{:S(2)}) collective-permute-start(bf16[1024,256]{1,0:T(8,128)(2,1)S(1)} %all_gather.3), channel_id=1, source_target_pairs={{0,64},{8,72},{16,80},{24,88},{32,96},{40,104},{48,112},{56,120},{... | collective-permute-start | bytes 1572872 | tf_op jit(solution)/shard_map/ppermute | solution.py:9
  103.1 50.5 %copy-start.16 = (s32[96,2]{0,1:T(2,128)S(1)}, s32[96,2]{0,1:T(2,128)}, u32[]{:S(2)}) copy-start(s32[96,2]{0,1:T(2,128)} %param.10) | copy-start | bytes 2308
  103.2 50.5 %copy-start.5 = (s32[1,8]{1,0:T(1,128)S(1)}, s32[1,8]{1,0:T(1,128)}, u32[]{:S(2)}) copy-start(s32[1,8]{1,0:T(1,128)} %param.11) | copy-start | bytes 100
  116.0 34.8 %collective-permute-start.1 = (bf16[1024,256]{1,0:T(8,128)(2,1)S(1)}, bf16[1024,256]{1,0:T(8,128)(2,1)S(1)}, u32[]{:S(2)}, u32[]{:S(2)}) collective-permute-start(bf16[1024,256]{1,0:T(8,128)(2,1)S(1)} %broadcast_select_fusion), channel_id=1, source_target_pairs={{0,128},{8,136},{16,144},{24,152},{32,160},{40,168},{48,176},{56,1... | collective-permute-start | bytes 1572872 | tf_op jit(solution)/shard_map/ppermute | solution.py:9
  150.9 22.2 %collective-permute-start.2 = (bf16[1024,256]{1,0:T(8,128)(2,1)S(1)}, bf16[1024,256]{1,0:T(8,128)(2,1)S(1)}, u32[]{:S(2)}, u32[]{:S(2)}) collective-permute-start(bf16[1024,256]{1,0:T(8,128)(2,1)S(1)} %broadcast_select_fusion.1), channel_id=1, source_target_pairs={{0,256},{8,264},{16,272},{24,280},{32,288},{40,296},{48,304},{56,3... | collective-permute-start | bytes 1572872 | tf_op jit(solution)/shard_map/ppermute | solution.py:9
  173.2 12.9 %collective-permute-start.3 = (bf16[1024,256]{1,0:T(8,128)(2,1)S(1)}, bf16[1024,256]{1,0:T(8,128)(2,1)S(1)}, u32[]{:S(2)}, u32[]{:S(2)}) collective-permute-start(bf16[1024,256]{1,0:T(8,128)(2,1)S(1)} %broadcast_select_fusion.2), channel_id=1, source_target_pairs={{0,8},{8,16},{16,24},{24,32},{32,40},{40,48},{48,56},{56,64},{64,7... | collective-permute-start | bytes 1572872 | tf_op jit(solution)/shard_map/ppermute | solution.py:9
  186.1 32.9 %copy-start.2 = (bf16[1024,256]{1,0:T(8,128)(2,1)}, bf16[1024,256]{1,0:T(8,128)(2,1)S(1)}, u32[]{:S(2)}) copy-start(bf16[1024,256]{1,0:T(8,128)(2,1)S(1)} %collective-permute-done.3) | copy-start | bytes 1572868
  186.1 10.5 %collective-permute-start.4 = (bf16[1024,256]{1,0:T(8,128)(2,1)S(1)}, bf16[1024,256]{1,0:T(8,128)(2,1)S(1)}, u32[]{:S(2)}, u32[]{:S(2)}) collective-permute-start(bf16[1024,256]{1,0:T(8,128)(2,1)S(1)} %collective-permute-done.3), channel_id=1, source_target_pairs={{0,8},{8,16},{16,24},{24,32},{32,40},{40,48},{48,56},{56,64},{64,7... | collective-permute-start | bytes 1572872 | tf_op jit(solution)/shard_map/ppermute | solution.py:9
  196.5 19.2 %copy-start.3 = (bf16[1024,256]{1,0:T(8,128)(2,1)}, bf16[1024,256]{1,0:T(8,128)(2,1)S(1)}, u32[]{:S(2)}) copy-start(bf16[1024,256]{1,0:T(8,128)(2,1)S(1)} %collective-permute-done.4) | copy-start | bytes 1572868
  196.6 15.6 %collective-permute-start.5 = (bf16[1024,256]{1,0:T(8,128)(2,1)S(1)}, bf16[1024,256]{1,0:T(8,128)(2,1)}, u32[]{:S(2)}, u32[]{:S(2)}) collective-permute-start(bf16[1024,256]{1,0:T(8,128)(2,1)S(1)} %collective-permute-done.4), channel_id=1, source_target_pairs={{0,8},{8,16},{16,24},{24,32},{32,40},{40,48},{48,56},{56,64},{64,7... | collective-permute-start | bytes 1572872 | tf_op jit(solution)/shard_map/ppermute | solution.py:9
  212.1 19.5 %collective-permute-start.6 = (bf16[1024,256]{1,0:T(8,128)(2,1)}, bf16[1024,256]{1,0:T(8,128)(2,1)}, u32[]{:S(2)}, u32[]{:S(2)}) collective-permute-start(bf16[1024,256]{1,0:T(8,128)(2,1)} %collective-permute-done.5), channel_id=1, source_target_pairs={{0,8},{8,16},{16,24},{24,32},{32,40},{40,48},{48,56},{56,64},{64,7... | collective-permute-start | bytes 1572872 | tf_op jit(solution)/shard_map/ppermute | solution.py:9
  231.7 19.5 %collective-permute-start.7 = (bf16[1024,256]{1,0:T(8,128)(2,1)}, bf16[1024,256]{1,0:T(8,128)(2,1)}, u32[]{:S(2)}, u32[]{:S(2)}) collective-permute-start(bf16[1024,256]{1,0:T(8,128)(2,1)} %collective-permute-done.6), channel_id=1, source_target_pairs={{0,8},{8,16},{16,24},{24,32},{32,40},{40,48},{48,56},{56,64},{64,7... | collective-permute-start | bytes 1572872 | tf_op jit(solution)/shard_map/ppermute | solution.py:9
  235.1 1.6 copy-start.15
  236.7 3.1 copy-start.4
  242.1 1.6 copy-start.14
  251.2 19.5 %collective-permute-start.8 = (bf16[1024,256]{1,0:T(8,128)(2,1)}, bf16[1024,256]{1,0:T(8,128)(2,1)}, u32[]{:S(2)}, u32[]{:S(2)}) collective-permute-start(bf16[1024,256]{1,0:T(8,128)(2,1)} %collective-permute-done.7), channel_id=1, source_target_pairs={{0,8},{8,16},{16,24},{24,32},{32,40},{40,48},{48,56},{56,64},{64,7... | collective-permute-start | bytes 1572872 | tf_op jit(solution)/shard_map/ppermute | solution.py:9
  254.8 1.6 copy-start.13
  262.7 1.6 copy-start.12
  267.4 5.2 %copy-start.8 = (pred[12]{0:T(512)(128)(4,1)S(1)}, pred[12]{0:T(512)(128)(4,1)}, u32[]{:S(2)}) copy-start(pred[12]{0:T(512)(128)(4,1)} %get-tuple-element.24) | copy-start | bytes 40
  270.7 19.5 %collective-permute-start.9 = (bf16[1024,256]{1,0:T(8,128)(2,1)}, bf16[1024,256]{1,0:T(8,128)(2,1)}, u32[]{:S(2)}, u32[]{:S(2)}) collective-permute-start(bf16[1024,256]{1,0:T(8,128)(2,1)} %collective-permute-done.8), channel_id=1, source_target_pairs={{0,8},{8,16},{16,24},{24,32},{32,40},{40,48},{48,56},{56,64},{64,7... | collective-permute-start | bytes 1572872 | tf_op jit(solution)/shard_map/ppermute | solution.py:9
  274.1 1.6 copy-start.11
  278.9 1.7 copy-start.7
  278.9 1.7 copy-start.17
  282.1 1.6 copy-start.10
  286.8 5.0 %copy-start.6 = (pred[12]{0:T(512)(128)(4,1)S(1)}, pred[12]{0:T(512)(128)(4,1)}, u32[]{:S(2)}) copy-start(pred[12]{0:T(512)(128)(4,1)} %get-tuple-element.6) | copy-start | bytes 40
  286.8 5.0 %copy-start.18 = (f32[12]{0:T(128)S(1)}, f32[12]{0:T(128)}, u32[]{:S(2)}) copy-start(f32[12]{0:T(128)} %compare_convert_fusion) | copy-start | bytes 148
  294.5 1.9 copy-start.9
  298.3 1.0 copy-start.1
Sparse Core Ops, SparseCore 0:
  299.4 147.2 reduce-scatter.1
where the time goes:
time: 456 us; the launch traced here: 455 us
  waiting for transfers between devices  246 us (54%)
  blocking collectives  90.3 us (20%)
  other arithmetic  34.3 us (8%)
  starting transfers between devices  28.5 us (6%)
  local copies, waits for them, and re-layouts  26.7 us (6%)
  matrix products  15.9 us (3%)
  between operations  13.9 us (3%)
    reduce_scatter x1, waiting for transfers between devices, local(): lax.psum_scatter(running.reshape(block_count * tile_size, feat_width), 'r...  147 us
    ppermute x10, waiting for transfers between devices, from_behind(): return lax.ppermute(x, axis, [(i, (i + by) % count) for i in range(count)])  98.2 us
    all_gather x1, blocking collectives, local(): current_slab = lax.all_gather(features, 'rep', axis=0, tiled=True)  90.3 us
    ppermute x10, starting transfers between devices, from_behind(): return lax.ppermute(x, axis, [(i, (i + by) % count) for i in range(count)])  28.5 us
    scatter-add x8, other arithmetic, local(): running.at[coords[step_index, :, 0]]  22.4 us
    dot_general x8, matrix products, local(): jnp.einsum('ktc,kcf->ktf', values[step_index], pieces, preferred_element_...  14.2 us
    mul x8, local copies, waits for them, and re-layouts, local(): products * live_slot[:, None, None]  13.5 us
    gather x8, local copies, waits for them, and re-layouts, local(): pieces = jnp.take(slab_blocks, coords[step_index, :, 1], axis=0)  11.4 us
  transfers between devices with their start and end apart: 11, of which 11 were waited for; matrix products, arithmetic and copies ran while one was open for 15% of the time, Pallas kernels for 0%

commit v1 on v0

--- a/solution.py
+++ b/solution.py
@@ -16,7 +16,9 @@
     tile_size = tile_values.shape[1]
     feat_width = features.shape[1]
     slot_count = tile_values.shape[0] // step_count
-    current_slab = lax.all_gather(features, "rep", axis=0, tiled=True)
+    current_slab = jnp.concatenate(
+        lax.all_to_all(jnp.stack([features] * lax.axis_size("rep")), "rep", 0, 0), axis=0
+    )
     block_count = current_slab.shape[0] // tile_size
     values = tile_values.reshape(step_count, slot_count, tile_size, tile_size)
     coords = tile_coords.reshape(step_count, slot_count, 2)

time: 456 us -> 418 us (0.917)
  the two profiles are of different devices: /device:TPU:2 before, /device:TPU:6 now
where the time goes in v1:
time: 418 us; the launch traced here: 416 us
  waiting for transfers between devices  242 us (58%)
  starting transfers between devices  45.8 us (11%)
  blocking collectives  36.8 us (9%)
  other arithmetic  34.4 us (8%)
  local copies, waits for them, and re-layouts  27.6 us (7%)
  matrix products  15.9 us (4%)
  between operations  14 us (3%)
    reduce_scatter x1, waiting for transfers between devices, local(): lax.psum_scatter(running.reshape(block_count * tile_size, feat_width), 'r...  147 us
    ppermute x10, waiting for transfers between devices, from_behind(): return lax.ppermute(x, axis, [(i, (i + by) % count) for i in range(count)])  95 us
    ppermute x10, starting transfers between devices, from_behind(): return lax.ppermute(x, axis, [(i, (i + by) % count) for i in range(count)])  45.8 us
    all_to_all x1, blocking collectives, local(): lax.all_to_all(jnp.stack([features] * lax.axis_size('rep')), 'rep', 0, 0)  36.8 us
    scatter-add x8, other arithmetic, local(): running.at[coords[step_index, :, 0]]  22.4 us
    dot_general x8, matrix products, local(): jnp.einsum('ktc,kcf->ktf', values[step_index], pieces, preferred_element_...  14.2 us
    mul x8, local copies, waits for them, and re-layouts, local(): products * live_slot[:, None, None]  13.5 us
    gather x8, local copies, waits for them, and re-layouts, local(): pieces = jnp.take(slab_blocks, coords[step_index, :, 1], axis=0)  11.4 us
  transfers between devices with their start and end apart: 11, of which 7 were waited for; matrix products, arithmetic and copies ran while one was open for 16% of the time, Pallas kernels for 0%

profile of v1, /device:TPU:6, one launch (start us, length us, event | category | flops | bytes accessed | tf_op | source)
XLA Modules:
  0.0 416.3 jit_solution(17111508761935468788)
XLA Ops:
  6.5 0.9 stack.2
  7.5 36.8 %all_to_all.5 = bf16[8,128,256]{2,1,0:T(8,128)(2,1)S(1)} all-to-all(bf16[8,128,256]{2,1,0:T(8,128)(2,1)S(1)} %stack.2), channel_id=1, replica_groups=mesh['loop'=64,'rep'=8] {'rep'}, dimensions={0} | all-to-all | bytes 1048576 | tf_op jit(solution)/shard_map/all_to_all | solution.py:20
  44.3 19.4 %collective-permute-start = (bf16[1024,256]{1,0:T(8,128)(2,1)S(1)}, bf16[1024,256]{1,0:T(8,128)(2,1)S(1)}, u32[]{:S(2)}, u32[]{:S(2)}) collective-permute-start(bf16[1024,256]{1,0:T(8,128)(2,1)S(1)} %bitcast.160), channel_id=1, source_target_pairs={{0,64},{8,72},{16,80},{24,88},{32,96},{40,104},{48,112},{56,120},{... | collective-permute-start | bytes 1572872 | tf_op jit(solution)/shard_map/ppermute | solution.py:9
  63.7 10.1 %collective-permute-done = bf16[1024,256]{1,0:T(8,128)(2,1)S(1)} collective-permute-done((bf16[1024,256]{1,0:T(8,128)(2,1)S(1)}, bf16[1024,256]{1,0:T(8,128)(2,1)S(1)}, u32[]{:S(2)}, u32[]{:S(2)}) %collective-permute-start) | collective-permute-done | bytes 524320 | tf_op jit(solution)/shard_map/ppermute | solution.py:9
  73.9 4.1 collective-permute-start.1
  78.0 26.5 %collective-permute-done.1 = bf16[1024,256]{1,0:T(8,128)(2,1)S(1)} collective-permute-done((bf16[1024,256]{1,0:T(8,128)(2,1)S(1)}, bf16[1024,256]{1,0:T(8,128)(2,1)S(1)}, u32[]{:S(2)}, u32[]{:S(2)}) %collective-permute-start.1) | collective-permute-done | bytes 524320 | tf_op jit(solution)/shard_map/ppermute | solution.py:9
  104.5 1.9 collective-permute-start.2
  106.6 0.7 fusion.50
  107.3 0.6 compare_convert_fusion.7
  107.9 1.2 compare_convert_fusion.6
  109.1 40.8 %collective-permute-done.2 = bf16[1024,256]{1,0:T(8,128)(2,1)S(1)} collective-permute-done((bf16[1024,256]{1,0:T(8,128)(2,1)S(1)}, bf16[1024,256]{1,0:T(8,128)(2,1)S(1)}, u32[]{:S(2)}, u32[]{:S(2)}) %collective-permute-start.2) | collective-permute-done | bytes 524320 | tf_op jit(solution)/shard_map/ppermute | solution.py:9
  149.9 1.9 collective-permute-start.3
  151.9 1.2 compare_convert_fusion.5
  153.1 1.1 compare_convert_fusion.4
  154.2 1.2 compare_convert_fusion.3
  155.4 0.6 compare_and_fusion
  156.0 4.4 %collective-permute-done.3 = bf16[1024,256]{1,0:T(8,128)(2,1)S(1)} collective-permute-done((bf16[1024,256]{1,0:T(8,128)(2,1)S(1)}, bf16[1024,256]{1,0:T(8,128)(2,1)S(1)}, u32[]{:S(2)}, u32[]{:S(2)}) %collective-permute-start.3) | collective-permute-done | bytes 524320 | tf_op jit(solution)/shard_map/ppermute | solution.py:9
  160.4 1.9 collective-permute-start.4
  162.4 1.2 compare_convert_fusion.2
  163.6 0.6 pad_clamp_fusion.6
  165.3 5.6 %collective-permute-done.4 = bf16[1024,256]{1,0:T(8,128)(2,1)S(1)} collective-permute-done((bf16[1024,256]{1,0:T(8,128)(2,1)S(1)}, bf16[1024,256]{1,0:T(8,128)(2,1)S(1)}, u32[]{:S(2)}, u32[]{:S(2)}) %collective-permute-start.4) | collective-permute-done | bytes 524320 | tf_op jit(solution)/shard_map/ppermute | solution.py:9
  170.9 1.9 collective-permute-start.5
  172.9 1.1 compare_convert_fusion.1
  174.0 7.5 %collective-permute-done.5 = bf16[1024,256]{1,0:T(8,128)(2,1)} collective-permute-done((bf16[1024,256]{1,0:T(8,128)(2,1)S(1)}, bf16[1024,256]{1,0:T(8,128)(2,1)}, u32[]{:S(2)}, u32[]{:S(2)}) %collective-permute-start.5) | collective-permute-done | bytes 524320 | tf_op jit(solution)/shard_map/ppermute | solution.py:9
  181.5 3.6 collective-permute-start.6
  185.1 1.1 compare_convert_fusion
  186.2 0.6 fusion.41
  187.4 2.6 multiply_bitcast_fusion.7
  190.1 1.9 copy.33
  192.0 1.8 scatter_fusion
  193.9 1.8 gather_fusion.1
  195.7 6.6 %collective-permute-start.7 = (bf16[1024,256]{1,0:T(8,128)(2,1)}, bf16[1024,256]{1,0:T(8,128)(2,1)}, u32[]{:S(2)}, u32[]{:S(2)}) collective-permute-start(bf16[1024,256]{1,0:T(8,128)(2,1)} %collective-permute-done.6), channel_id=1, source_target_pairs={{0,8},{8,16},{16,24},{24,32},{32,40},{40,48},{48,56},{56,64},{64,7... | collective-permute-start | bytes 1572872 | tf_op jit(solution)/shard_map/ppermute | solution.py:9
  202.3 1.5 multiply_bitcast_fusion.6
  203.8 1.6 copy.37
  205.4 3.1 scatter_fusion.1
  208.5 0.7 gather_fusion.2
  209.3 1.5 multiply_bitcast_fusion.5
  210.8 1.6 copy.41
  212.4 3.1 scatter_fusion.2
  215.5 1.8 gather_fusion.3
  217.3 2.5 collective-permute-start.8
  219.8 1.5 multiply_bitcast_fusion.4
  221.3 1.6 copy.45
  222.9 3.1 scatter_fusion.3
  226.1 1.6 gather_fusion.4
  227.7 1.5 multiply_bitcast_fusion.3
  229.2 1.6 copy.49
  230.8 3.1 scatter_fusion.4
  234.0 1.6 gather_fusion.5
  235.6 1.9 collective-permute-start.9
  237.6 1.5 multiply_bitcast_fusion.2
  239.1 1.6 copy.53
  240.7 3.1 scatter_fusion.5
  243.9 1.6 gather_fusion.6
  245.5 1.5 multiply_bitcast_fusion.1
  247.0 1.6 copy.57
  248.7 3.1 scatter_fusion.6
  251.8 1.6 gather_fusion.7
  253.5 2.6 multiply_bitcast_fusion
  256.1 1.9 copy.61
  258.0 1.8 scatter_fusion.7
  259.9 1.0 copy-done.1
  260.8 147.0 %reduce-scatter.2.cloned.1.call-done = f32[128,256]{1,0:T(8,128)} async-done(((f32[1024,256]{1,0:T(8,128)}), f32[128,256]{1,0:T(8,128)}) %reduce-scatter.2.cloned.1.call-update) | async-done | bytes 131088 | tf_op jit(solution)/shard_map/reduce_scatter | solution.py:41
  407.8 1.7 fusion
  (56 shorter events, 2.3 us)
Async XLA Ops:
  6.5 401.3 %copy-start = (bf16[256,256]{1,0:T(8,128)(2,1)S(1)}, bf16[256,256]{1,0:T(8,128)(2,1)}, u32[]{:S(2)}) copy-start(bf16[256,256]{1,0:T(8,128)(2,1)} %param.8) | copy-start | bytes 393220
  6.5 401.3 %reduce-scatter.2.cloned.1.call-start = ((), (), s32[]{:S(2)}) async-start(), calls=%async_computation.2 | async-start | bytes 1179648 | tf_op jit(solution)/shard_map/reduce_scatter | solution.py:41
  44.3 29.5 %collective-permute-start = (bf16[1024,256]{1,0:T(8,128)(2,1)S(1)}, bf16[1024,256]{1,0:T(8,128)(2,1)S(1)}, u32[]{:S(2)}, u32[]{:S(2)}) collective-permute-start(bf16[1024,256]{1,0:T(8,128)(2,1)S(1)} %bitcast.160), channel_id=1, source_target_pairs={{0,64},{8,72},{16,80},{24,88},{32,96},{40,104},{48,112},{56,120},{... | collective-permute-start | bytes 1572872 | tf_op jit(solution)/shard_map/ppermute | solution.py:9
  63.6 42.8 %copy-start.16 = (s32[96,2]{0,1:T(2,128)S(1)}, s32[96,2]{0,1:T(2,128)}, u32[]{:S(2)}) copy-start(s32[96,2]{0,1:T(2,128)} %param.10) | copy-start | bytes 2308
  63.7 42.9 %copy-start.5 = (s32[1,8]{1,0:T(1,128)S(1)}, s32[1,8]{1,0:T(1,128)}, u32[]{:S(2)}) copy-start(s32[1,8]{1,0:T(1,128)} %param.11) | copy-start | bytes 100
  73.9 30.6 %collective-permute-start.1 = (bf16[1024,256]{1,0:T(8,128)(2,1)S(1)}, bf16[1024,256]{1,0:T(8,128)(2,1)S(1)}, u32[]{:S(2)}, u32[]{:S(2)}) collective-permute-start(bf16[1024,256]{1,0:T(8,128)(2,1)S(1)} %broadcast_select_fusion), channel_id=1, source_target_pairs={{0,128},{8,136},{16,144},{24,152},{32,160},{40,168},{48,176},{56,1... | collective-permute-start | bytes 1572872 | tf_op jit(solution)/shard_map/ppermute | solution.py:9
  104.5 45.3 %collective-permute-start.2 = (bf16[1024,256]{1,0:T(8,128)(2,1)S(1)}, bf16[1024,256]{1,0:T(8,128)(2,1)S(1)}, u32[]{:S(2)}, u32[]{:S(2)}) collective-permute-start(bf16[1024,256]{1,0:T(8,128)(2,1)S(1)} %broadcast_select_fusion.1), channel_id=1, source_target_pairs={{0,256},{8,264},{16,272},{24,280},{32,288},{40,296},{48,304},{56,3... | collective-permute-start | bytes 1572872 | tf_op jit(solution)/shard_map/ppermute | solution.py:9
  149.9 10.5 %collective-permute-start.3 = (bf16[1024,256]{1,0:T(8,128)(2,1)S(1)}, bf16[1024,256]{1,0:T(8,128)(2,1)S(1)}, u32[]{:S(2)}, u32[]{:S(2)}) collective-permute-start(bf16[1024,256]{1,0:T(8,128)(2,1)S(1)} %broadcast_select_fusion.2), channel_id=1, source_target_pairs={{0,8},{8,16},{16,24},{24,32},{32,40},{40,48},{48,56},{56,64},{64,7... | collective-permute-start | bytes 1572872 | tf_op jit(solution)/shard_map/ppermute | solution.py:9
  160.4 29.6 %copy-start.2 = (bf16[1024,256]{1,0:T(8,128)(2,1)}, bf16[1024,256]{1,0:T(8,128)(2,1)S(1)}, u32[]{:S(2)}) copy-start(bf16[1024,256]{1,0:T(8,128)(2,1)S(1)} %collective-permute-done.3) | copy-start | bytes 1572868
  160.4 10.5 %collective-permute-start.4 = (bf16[1024,256]{1,0:T(8,128)(2,1)S(1)}, bf16[1024,256]{1,0:T(8,128)(2,1)S(1)}, u32[]{:S(2)}, u32[]{:S(2)}) collective-permute-start(bf16[1024,256]{1,0:T(8,128)(2,1)S(1)} %collective-permute-done.3), channel_id=1, source_target_pairs={{0,8},{8,16},{16,24},{24,32},{32,40},{40,48},{48,56},{56,64},{64,7... | collective-permute-start | bytes 1572872 | tf_op jit(solution)/shard_map/ppermute | solution.py:9
  170.9 15.9 %copy-start.3 = (bf16[1024,256]{1,0:T(8,128)(2,1)}, bf16[1024,256]{1,0:T(8,128)(2,1)S(1)}, u32[]{:S(2)}) copy-start(bf16[1024,256]{1,0:T(8,128)(2,1)S(1)} %collective-permute-done.4) | copy-start | bytes 1572868
  170.9 10.6 %collective-permute-start.5 = (bf16[1024,256]{1,0:T(8,128)(2,1)S(1)}, bf16[1024,256]{1,0:T(8,128)(2,1)}, u32[]{:S(2)}, u32[]{:S(2)}) collective-permute-start(bf16[1024,256]{1,0:T(8,128)(2,1)S(1)} %collective-permute-done.4), channel_id=1, source_target_pairs={{0,8},{8,16},{16,24},{24,32},{32,40},{40,48},{48,56},{56,64},{64,7... | collective-permute-start | bytes 1572872 | tf_op jit(solution)/shard_map/ppermute | solution.py:9
  181.5 14.1 %collective-permute-start.6 = (bf16[1024,256]{1,0:T(8,128)(2,1)}, bf16[1024,256]{1,0:T(8,128)(2,1)}, u32[]{:S(2)}, u32[]{:S(2)}) collective-permute-start(bf16[1024,256]{1,0:T(8,128)(2,1)} %collective-permute-done.5), channel_id=1, source_target_pairs={{0,8},{8,16},{16,24},{24,32},{32,40},{40,48},{48,56},{56,64},{64,7... | collective-permute-start | bytes 1572872 | tf_op jit(solution)/shard_map/ppermute | solution.py:9
  195.7 21.6 %collective-permute-start.7 = (bf16[1024,256]{1,0:T(8,128)(2,1)}, bf16[1024,256]{1,0:T(8,128)(2,1)}, u32[]{:S(2)}, u32[]{:S(2)}) collective-permute-start(bf16[1024,256]{1,0:T(8,128)(2,1)} %collective-permute-done.6), channel_id=1, source_target_pairs={{0,8},{8,16},{16,24},{24,32},{32,40},{40,48},{48,56},{56,64},{64,7... | collective-permute-start | bytes 1572872 | tf_op jit(solution)/shard_map/ppermute | solution.py:9
  203.8 1.6 copy-start.15
  205.4 3.1 copy-start.4
  210.8 1.6 copy-start.14
  217.3 18.3 %collective-permute-start.8 = (bf16[1024,256]{1,0:T(8,128)(2,1)}, bf16[1024,256]{1,0:T(8,128)(2,1)}, u32[]{:S(2)}, u32[]{:S(2)}) collective-permute-start(bf16[1024,256]{1,0:T(8,128)(2,1)} %collective-permute-done.7), channel_id=1, source_target_pairs={{0,8},{8,16},{16,24},{24,32},{32,40},{40,48},{48,56},{56,64},{64,7... | collective-permute-start | bytes 1572872 | tf_op jit(solution)/shard_map/ppermute | solution.py:9
  221.3 1.6 copy-start.13
  229.2 1.6 copy-start.12
  234.0 3.6 copy-start.8
  235.6 16.2 %collective-permute-start.9 = (bf16[1024,256]{1,0:T(8,128)(2,1)}, bf16[1024,256]{1,0:T(8,128)(2,1)}, u32[]{:S(2)}, u32[]{:S(2)}) collective-permute-start(bf16[1024,256]{1,0:T(8,128)(2,1)} %collective-permute-done.8), channel_id=1, source_target_pairs={{0,8},{8,16},{16,24},{24,32},{32,40},{40,48},{48,56},{56,64},{64,7... | collective-permute-start | bytes 1572872 | tf_op jit(solution)/shard_map/ppermute | solution.py:9
  239.1 1.6 copy-start.11
  243.8 1.7 copy-start.7
  243.9 1.7 copy-start.17
  247.0 1.6 copy-start.10
  251.8 1.7 copy-start.6
  251.8 1.7 copy-start.18
  256.1 1.9 copy-start.9
  259.8 1.0 copy-start.1
Sparse Core Ops, SparseCore 0:
  261.0 146.7 reduce-scatter.1
